TPU v7x, 128 devices: a whole 4x4x4 slice. The times are simulated.
128 devices in a mesh: seq: 16 (over z, x), head: 8 (over y, core).
Axes of the slice: x: 4, y: 4, z: 4, core: 2. Of those that a mesh axis runs over, the one named last changes fastest.
Arguments:
- query: bfloat16 [8192, 4096], P(('seq', 'head')), may hold values from -41 to 41
- keys: bfloat16 [262144, 1024], P('seq', 'head'), may hold values from -14 to 14
- values: bfloat16 [262144, 1024], P('seq', 'head'), may hold values from -6 to 6
- out_grad: bfloat16 [8192, 4096], P(('seq', 'head')), may hold values from -6 to 6
- span_pos: int32 [16], P('seq'), may hold values from 1 to 31, as said below
- selected: int32 [16, 4], P('seq'), may hold values from -1 to 510, as said below
Outputs:
- attn_out: bfloat16 [8192, 4096], P(('seq', 'head'))
- query_grad: bfloat16 [8192, 4096], P(('seq', 'head'))
- key_grad: bfloat16 [262144, 1024], P('seq', 'head')
- value_grad: bfloat16 [262144, 1024], P('seq', 'head')
Inputs may be any that keep to these rules, and one draw needn't show every extreme that they name: `span_pos`: block index of the span's queries within its shard. `selected`: entry [s, j] is -1 if s < j; otherwise it indexes a block of shard s - j (blocks (s - j) * 32 onward), and for j = 0 one earlier than span s's own block s * 32 + span_pos[s].
All inputs are finite; a program needn't handle non-finite values.
Results may differ from a plain program's by a relative error of at most 0.029.
Values may be sent and summed in bfloat16 or wider, within the bound.
A program may use at most 128 MiB of HBM per device.

v0:
```python
import jax
import jax.numpy as jnp
from jax import lax
from jax.sharding import PartitionSpec as P

HEAD_DIM = 128


masked_score = -1e30


def shifted(value, axis, steps):
    count = lax.axis_size(axis)
    first, last = (max(0, -steps), min(count, count - steps))
    return lax.ppermute(value, axis, [(source, source + steps) for source in range(first, last)])


def forward(query_rows, key_rows, value_rows, allowed, score_scale):
    scores = (
        jnp.einsum("qhgd,khd->hgqk", query_rows, key_rows, preferred_element_type=jnp.float32)
        * score_scale
    )
    scores = jnp.where(allowed, scores, masked_score)
    row_max = jnp.max(scores, axis=-1, keepdims=True)
    exponent = jnp.exp(scores - row_max)
    weights = exponent / jnp.sum(exponent, axis=-1, keepdims=True)
    weights_low = weights.astype(jnp.bfloat16)
    attended = jnp.einsum(
        "hgqk,khd->qhgd", weights_low, value_rows, preferred_element_type=jnp.float32
    ).astype(jnp.bfloat16)
    return (weights, weights_low, attended)


def backward(
    query_rows, grad_rows, key_rows, value_rows, weights, weights_low, attended, score_scale
):
    row_delta = jnp.sum(grad_rows.astype(jnp.float32) * attended.astype(jnp.float32), axis=-1)
    weight_grad = jnp.einsum(
        "qhgd,khd->hgqk", grad_rows, value_rows, preferred_element_type=jnp.float32
    )
    score_grad = (weights * (weight_grad - jnp.transpose(row_delta, (1, 2, 0))[..., None])).astype(
        jnp.bfloat16
    )
    query_part = (
        jnp.einsum("hgqk,khd->qhgd", score_grad, key_rows, preferred_element_type=jnp.float32)
        * score_scale
    ).astype(jnp.bfloat16)
    key_part = (
        jnp.einsum("hgqk,qhgd->khd", score_grad, query_rows, preferred_element_type=jnp.float32)
        * score_scale
    ).astype(jnp.bfloat16)
    value_part = jnp.einsum(
        "hgqk,qhgd->khd", weights_low, grad_rows, preferred_element_type=jnp.float32
    ).astype(jnp.bfloat16)
    return (query_part, key_part, value_part)


def pair_block(keys, values, local_block, block_rows):
    start = local_block * block_rows
    return jnp.stack(
        [
            lax.dynamic_slice_in_dim(keys, start, block_rows, 0),
            lax.dynamic_slice_in_dim(values, start, block_rows, 0),
        ],
        0,
    )


def per_device(query, keys, values, out_grad, span_pos, selected):
    seq_count = lax.axis_size("seq")
    seq_index = lax.axis_index("seq")
    query_all, grad_all = (
        lax.all_to_all(query, "head", split_axis=1, concat_axis=0, tiled=True),
        lax.all_to_all(out_grad, "head", split_axis=1, concat_axis=0, tiled=True),
    )
    block_rows = query_all.shape[0]
    feature_width = keys.shape[1]
    local_heads = feature_width // HEAD_DIM
    group_size = query_all.shape[1] // feature_width
    shard_blocks = keys.shape[0] // block_rows
    picks = selected.shape[1]
    score_scale = HEAD_DIM ** (-0.5)
    from_above = [shifted(selected, "seq", -distance) for distance in range(1, picks)]
    wanted_local = []
    wanted_present = []
    outgoing = []
    for distance in range(1, picks):
        entry = from_above[distance - 1][0, distance]
        present = (seq_index + distance < seq_count) & (entry >= 0)
        local_block = jnp.clip(entry - seq_index * shard_blocks, 0, shard_blocks - 1)
        wanted_local.append(local_block)
        wanted_present.append(present)
        outgoing.append(pair_block(keys, values, local_block, block_rows))
    chosen = selected[0]
    usable = chosen >= 0
    first_local = jnp.clip(chosen[0] - seq_index * shard_blocks, 0, shard_blocks - 1)
    first_pair = pair_block(keys, values, first_local, block_rows)
    own_pair = pair_block(keys, values, span_pos[0], block_rows)
    rows_total = (picks + 1) * block_rows
    columns = jnp.arange(rows_total)
    query_pos = jnp.arange(block_rows)
    slot_of = columns // block_rows
    slot_ok = jnp.concatenate([usable, jnp.ones((1,), jnp.bool_)])[slot_of]
    allowed = jnp.where(
        slot_of[None, :] == picks,
        (columns % block_rows)[None, :] <= query_pos[:, None],
        slot_ok[None, :],
    )
    query_rows = query_all.reshape(block_rows, local_heads, group_size, HEAD_DIM)
    grad_rows = grad_all.reshape(block_rows, local_heads, group_size, HEAD_DIM)

    def assemble(arrived):
        stacked = jnp.concatenate(
            [first_pair[:, None]] + [piece[:, None] for piece in arrived] + [own_pair[:, None]], 1
        )
        stacked = stacked.reshape(2, rows_total, local_heads, HEAD_DIM)
        return (stacked[0], stacked[1])

    arrived = [shifted(outgoing[distance - 1], "seq", distance) for distance in range(1, picks)]
    key_rows, value_rows = assemble(arrived)
    weights, weights_low, attended = forward(query_rows, key_rows, value_rows, allowed, score_scale)
    again = [shifted(outgoing[distance - 1], "seq", distance) for distance in range(1, picks)]
    key_rows, value_rows = assemble(again)
    weights, weights_low, recomputed = forward(
        query_rows, key_rows, value_rows, allowed, score_scale
    )
    query_part, key_part, value_part = backward(
        query_rows, grad_rows, key_rows, value_rows, weights, weights_low, attended, score_scale
    )
    key_parts = key_part.reshape(picks + 1, block_rows, feature_width)
    value_parts = value_part.reshape(picks + 1, block_rows, feature_width)
    grad_pairs = jnp.stack([key_parts, value_parts], 0)
    returned = [shifted(grad_pairs[:, distance], "seq", -distance) for distance in range(1, picks)]
    block_ids = jnp.arange(shard_blocks)
    targets = [block_ids == first_local]
    for distance in range(1, picks):
        targets.append((block_ids == wanted_local[distance - 1]) & wanted_present[distance - 1])
    targets.append(block_ids == span_pos[0])
    placing = jnp.stack(targets, 0).astype(jnp.bfloat16)
    contributions = jnp.stack([grad_pairs[:, 0]] + returned + [grad_pairs[:, picks]], 1)
    placed = jnp.einsum(
        "np,cnbw->cpbw", placing, contributions, preferred_element_type=jnp.float32
    ).astype(jnp.bfloat16)
    key_grad = placed[0].reshape(-1, feature_width)
    value_grad = placed[1].reshape(-1, feature_width)
    attended_flat = attended.reshape(block_rows, -1)
    query_flat = query_part.reshape(block_rows, -1)
    attn_out, query_grad = (
        lax.all_to_all(attended_flat, "head", split_axis=0, concat_axis=1, tiled=True),
        lax.all_to_all(query_flat, "head", split_axis=0, concat_axis=1, tiled=True),
    )
    return (attn_out, query_grad, key_grad, value_grad)


def solution(mesh):
    in_specs = (
        P(("seq", "head"), None),
        P("seq", "head"),
        P("seq", "head"),
        P(("seq", "head"), None),
        P("seq"),
        P("seq", None),
    )
    out_specs = (
        P(("seq", "head"), None),
        P(("seq", "head"), None),
        P("seq", "head"),
        P("seq", "head"),
    )
    return jax.shard_map(
        per_device, mesh=mesh, in_specs=in_specs, out_specs=out_specs, check_vma=False
    )
```

profile of v0, /device:TPU:109, one launch (start us, length us, event | category | flops | bytes accessed | tf_op | source)
XLA Modules:
  0.0 185.2 jit_solution(4843566044329907514)
XLA Ops:
  0.6 2.1 %collective-permute-start.2 = (s32[1,4]{1,0:T(1,128)}, s32[1,4]{1,0:T(1,128)S(1)}, u32[]{:S(2)}, u32[]{:S(2)}) collective-permute-start(s32[1,4]{1,0:T(1,128)} %param.11), channel_id=1, source_target_pairs={{16,0},{24,8},{32,16},{40,24},{48,32},{56,40},{64,48},{72,56},{80,... | collective-permute-start | bytes 56 | tf_op jit(solution)/shard_map/ppermute | solution.py:15
  2.8 3.6 %collective-permute-start = (s32[1,4]{1,0:T(1,128)}, s32[1,4]{1,0:T(1,128)S(1)}, u32[]{:S(2)}, u32[]{:S(2)}) collective-permute-start(s32[1,4]{1,0:T(1,128)} %param.11), channel_id=1, source_target_pairs={{8,0},{16,8},{24,16},{32,24},{40,32},{48,40},{56,48},{64,56},{72,6... | collective-permute-start | bytes 56 | tf_op jit(solution)/shard_map/ppermute | solution.py:15
  6.4 1.9 %collective-permute-start.4 = (s32[1,4]{1,0:T(1,128)}, s32[1,4]{1,0:T(1,128)S(1)}, u32[]{:S(2)}, u32[]{:S(2)}) collective-permute-start(s32[1,4]{1,0:T(1,128)} %param.11), channel_id=1, source_target_pairs={{24,0},{32,8},{40,16},{48,24},{56,32},{64,40},{72,48},{80,56},{88,... | collective-permute-start | bytes 56 | tf_op jit(solution)/shard_map/ppermute | solution.py:15
  8.3 1.9 %copy.93 = bf16[8,8,8,512]{3,2,0,1:T(8,128)(2,1)} copy(bf16[8,8,8,512]{3,2,1,0:T(8,128)(2,1)} %bitcast.201) | data formatting | bytes 1048576 | tf_op jit(solution)/shard_map/all_to_all | solution.py:74
  10.2 5.8 %all-to-all-start.2 = ((bf16[64,8,512]{2,0,1:T(8,128)(2,1)}), bf16[64,8,512]{2,0,1:T(8,128)(2,1)S(1)}, u32[]{:S(2)}, u32[]{:S(2)}) async-start(bf16[64,8,512]{2,0,1:T(8,128)(2,1)} %bitcast.181), calls=%async_computation.2 | async-start | bytes 1048576 | tf_op jit(solution)/shard_map/all_to_all | solution.py:74
  17.2 0.7 broadcast_compare_fusion
  17.9 0.7 fusion.49
  18.6 1.9 %copy.94 = bf16[8,8,8,512]{3,2,0,1:T(8,128)(2,1)} copy(bf16[8,8,8,512]{3,2,1,0:T(8,128)(2,1)} %bitcast.202) | data formatting | bytes 1048576 | tf_op jit(solution)/shard_map/all_to_all | solution.py:73
  20.5 2.6 %select_reduce_fusion = pred[2560]{0:T(1024)(128)(4,1)S(1)} fusion(pred[]{:T(512)} %bitcast.22, pred[]{:T(512)} %bitcast.23, pred[]{:T(512)} %bitcast.25, pred[]{:T(512)} %bitcast.24), kind=kLoop, calls=%fused_computation.61 | loop fusion | flops 48640 | bytes 2564 | tf_op jit(solution)/shard_map/gather | solution.py:103
  23.1 2.3 %fusion.11 = pred[512,2560]{0,1:T(8,128)(4,1)S(1)} fusion(s32[2560]{0:T(1024)S(1)} %fusion.35, pred[2560]{0:T(1024)(128)(4,1)S(1)} %select_reduce_fusion, pred[2560]{0:T(1024)(128)(4,1)S(1)} %fusion.41), kind=kLoop, calls=%fused_computation.16 | loop fusion | flops 2621440 | bytes 1326080 | tf_op jit(solution)/shard_map/jit(_where)/select_n | solution.py:104
  25.4 0.6 slice.46
  26.6 0.6 slice.45
  27.9 0.7 slice.47
  30.6 2.2 %dynamic-slice_bitcast_fusion = (bf16[1,512,128]{2,1,0:T(8,128)(2,1)S(1)}, bf16[1,512,128]{2,1,0:T(8,128)(2,1)S(1)}, bf16[1,512,128]{2,1,0:T(8,128)(2,1)S(1)}, b...) fusion(bf16[16384,128]{1,0:T(8,128)(2,1)} %param.8, ...), kind=kLoop, calls=%fused_computation.50 | loop fusion | bytes 2621460 | tf_op jit(solution)/shard_map/stack | solution.py:60
  32.8 0.7 pad_maximum_fusion
  33.5 4.8 %collective-permute-start.1 = (bf16[2,512,128]{2,1,0:T(8,128)(2,1)}, bf16[2,512,128]{2,1,0:T(8,128)(2,1)}, u32[]{:S(2)}, u32[]{:S(2)}) collective-permute-start(bf16[2,512,128]{2,1,0:T(8,128)(2,1)} %pad_maximum_fusion), channel_id=1, source_target_pairs={{0,8},{8,16},{16,24},{24,32},{32,40},{40,48},{48,56},{56,64},{64,7... | collective-permute-start | bytes 786440 | tf_op jit(solution)/shard_map/ppermute | solution.py:15
  38.3 0.7 pad_maximum_fusion.1
  39.1 1.3 collective-permute-start.3
  40.4 0.7 pad_maximum_fusion.2
  41.1 1.3 collective-permute-start.5
  43.1 1.0 fusion.33
  44.2 1.0 bitcast_dynamic-update-slice_fusion.2
  45.1 4.8 %collective-permute-done.3 = bf16[2,512,128]{2,1,0:T(8,128)(2,1)} collective-permute-done((bf16[2,512,128]{2,1,0:T(8,128)(2,1)}, bf16[2,512,128]{2,1,0:T(8,128)(2,1)}, u32[]{:S(2)}, u32[]{:S(2)}) %collective-permute-start.3) | collective-permute-done | bytes 262176 | tf_op jit(solution)/shard_map/ppermute | solution.py:15
  50.0 1.0 bitcast_dynamic-update-slice_fusion.1
  51.0 2.9 %collective-permute-done.5 = bf16[2,512,128]{2,1,0:T(8,128)(2,1)} collective-permute-done((bf16[2,512,128]{2,1,0:T(8,128)(2,1)}, bf16[2,512,128]{2,1,0:T(8,128)(2,1)}, u32[]{:S(2)}, u32[]{:S(2)}) %collective-permute-start.5) | collective-permute-done | bytes 262176 | tf_op jit(solution)/shard_map/ppermute | solution.py:15
  53.8 1.0 bitcast_dynamic-update-slice_fusion
  54.9 6.0 %all-to-all-start = ((bf16[64,8,512]{2,0,1:T(8,128)(2,1)}), bf16[64,8,512]{2,0,1:T(8,128)(2,1)}, u32[]{:S(2)}, u32[]{:S(2)}) async-start(bf16[64,8,512]{2,0,1:T(8,128)(2,1)} %bitcast.182), calls=%async_computation | async-start | bytes 1048576 | tf_op jit(solution)/shard_map/all_to_all | solution.py:73
  60.8 1.2 fusion.48
  62.0 1.1 bitcast_convert_fusion
  63.1 1.6 reshape.232
  64.7 1.3 copy.48
  66.0 3.2 %all-to-all-done = bf16[64,8,512]{2,0,1:T(8,128)(2,1)} async-done(((bf16[64,8,512]{2,0,1:T(8,128)(2,1)}), bf16[64,8,512]{2,0,1:T(8,128)(2,1)}, u32[]{:S(2)}, u32[]{:S(2)}) %all-to-all-start) | async-done | bytes 524320 | tf_op jit(solution)/shard_map/all_to_all | solution.py:73
  69.2 1.2 reshape.228
  70.4 1.0 reshape.230
  71.3 5.0 %fusion.4 = (f32[4,512]{1,0:T(4,128)S(1)}, f32[2560,512,4]{1,0,2:T(8,128)S(1)}) fusion(pred[512,2560]{0,1:T(8,128)(4,1)S(1)} %fusion.11, bf16[2560,128,1]{1,0,2:T(8,128)(2,1)} %bitcast.194, bf16[512,4,128]{2,1,0:T(4,128)(2,1)S(1)} %reshape.228), kind=kOutput, calls=%fused_computation.7 | convolution fusion | flops 1357903872 | bytes 23470080 | tf_op jit(solution)/shard_map/qhgd,khd->hgqk/dot_general | solution.py:20
  76.3 4.5 %fusion.3 = f32[4,512]{1,0:T(4,128)S(1)} fusion(f32[2560,512,4]{1,0,2:T(8,128)S(1)} %get-tuple-element.28, f32[4,512]{1,0:T(4,128)S(1)} %get-tuple-element.27, pred[512,2560]{0,1:T(8,128)(4,1)S(1)} %fusion.11), kind=kLoop, calls=%fused_computation.6 | loop fusion | flops 20969472 | bytes 22298624 | tf_op jit(solution)/shard_map/reduce_sum | solution.py:26
  80.9 8.2 %fusion.17 = bf16[2560,128]{1,0:T(8,128)(2,1)} fusion(bf16[512,4,128]{2,1,0:T(4,128)(2,1)} %reshape.230, f32[4,512]{1,0:T(4,128)S(1)} %fusion.3, f32[4,512]{1,0:T(4,128)S(1)} %get-tuple-element.27, f32[2560,512,4]{1,0,2:T(8,128)S(1)} %get-tuple-element.28, pred[512,2560]{0,1:T(8,128)(4,1)S(1)} %fusion.11), kind=kOutput, calls=%fused_computation.21 | convolution fusion | flops 1368719360 | bytes 23478272 | tf_op jit(solution)/shard_map/hgqk,qhgd->khd/dot_general | solution.py:52
  89.1 6.9 %multiply_reduce_fusion = (f32[512,4]{0,1:T(4,128)S(1)}, bf16[512,1,4,128]{0,3,2,1:T(8,128)(2,1)}) fusion(f32[512,1,4,128]{0,3,2,1:T(8,128)S(1)} %copy-done.2, bf16[2560,128,1]{1,0,2:T(8,128)(2,1)S(1)} %bitcast.197, f32[4,512]{1,0:T(4,128)S(1)} %fusion.3, f32[4,512]{1,0:T(4,128)S(1)} %get-tuple-element.27, f32[2560,512,4]{1,0,2:T(8,128)S(1)} %get-tuple-element.28, ...), kind=kOutput, calls=%fused_computation.29 | convolution fusion | flops 1369438208 | bytes 24535040 | tf_op jit(solution)/shard_map/hgqk,khd->qhgd/dot_general | solution.py:28
  95.9 15.7 %fusion.5 = bf16[4,512,2560]{1,2,0:T(8,128)(2,1)} fusion(f32[4,512]{1,0:T(4,128)S(1)} %bitcast.209, f32[4,512]{1,0:T(4,128)S(1)} %fusion.3, f32[4,512]{1,0:T(4,128)S(1)} %get-tuple-element.27, f32[2560,512,4]{1,0,2:T(8,128)} %copy-done, pred[512,2560]{0,1:T(8,128)(4,1)S(1)} %fusion.11, bf16[2560,128,1]{1,0,2:T(8,128)(2,1)S(1)} %bitcast.198, ...), kind=kOutput, calls=%fused_computation.8 | convolution fusion | flops 1378877440 | bytes 33972224 | tf_op jit(solution)/shard_map/qhgd,khd->hgqk/dot_general | solution.py:38
  111.7 7.0 %fusion.16 = bf16[2560,128]{1,0:T(8,128)(2,1)S(1)} fusion(bf16[4,512,2560]{1,2,0:T(8,128)(2,1)} %fusion.5, bf16[512,4,128]{2,1,0:T(4,128)(2,1)S(1)} %copy-done.7), kind=kOutput, calls=%fused_computation.20 | convolution fusion | flops 1342832640 | bytes 11665408 | tf_op jit(solution)/shard_map/hgqk,qhgd->khd/dot_general | solution.py:49
  118.7 0.5 copy_dynamic-update-slice_fusion.1
  119.2 0.5 copy_dynamic-update-slice_fusion
  119.8 1.9 %fusion.47 = (bf16[2,1,512,128]{3,1,2,0:T(2,128)(2,1)S(1)}, bf16[2,1,512,128]{3,1,2,0:T(2,128)(2,1)S(1)}, bf16[2,1,512,128]{3,1,2,0:T(2,128)(2,1)S(1)}, bf16[2,1...) fusion(bf16[2,5,512,128]{3,1,2,0:T(8,128)(2,1)S(1)} %copy_dynamic-update-slice_fusion), kind=kLoop, calls=%fused_computation.87 | loop fusion | bytes 2621440 | tf_op jit(solution)/shard_map/slice | solution.py:140
  121.8 3.1 %collective-permute-start.6 = (bf16[2,512,128]{2,1,0:T(8,128)(2,1)S(1)}, bf16[2,512,128]{2,1,0:T(8,128)(2,1)S(1)}, u32[]{:S(2)}, u32[]{:S(2)}) collective-permute-start(bf16[2,512,128]{2,1,0:T(8,128)(2,1)S(1)} %bitcast.205), channel_id=1, source_target_pairs={{8,0},{16,8},{24,16},{32,24},{40,32},{48,40},{56,48},{64,56},{72,6... | collective-permute-start | bytes 786440 | tf_op jit(solution)/shard_map/ppermute | solution.py:15
  124.9 6.1 %collective-permute-start.7 = (bf16[2,512,128]{2,1,0:T(8,128)(2,1)S(1)}, bf16[2,512,128]{2,1,0:T(8,128)(2,1)}, u32[]{:S(2)}, u32[]{:S(2)}) collective-permute-start(bf16[2,512,128]{2,1,0:T(8,128)(2,1)S(1)} %bitcast.207), channel_id=1, source_target_pairs={{16,0},{24,8},{32,16},{40,24},{48,32},{56,40},{64,48},{72,56},{80,... | collective-permute-start | bytes 786440 | tf_op jit(solution)/shard_map/ppermute | solution.py:15
  131.0 0.7 copy.95
  131.7 3.5 %collective-permute-start.8 = (bf16[2,512,128]{2,1,0:T(8,128)(2,1)}, bf16[2,512,128]{2,1,0:T(8,128)(2,1)}, u32[]{:S(2)}, u32[]{:S(2)}) collective-permute-start(bf16[2,512,128]{2,1,0:T(8,128)(2,1)} %bitcast.183), channel_id=1, source_target_pairs={{24,0},{32,8},{40,16},{48,24},{56,32},{64,40},{72,48},{80,56},{88,... | collective-permute-start | bytes 786440 | tf_op jit(solution)/shard_map/ppermute | solution.py:15
  135.2 1.6 fusion.27
  136.8 0.3 copy.44
  137.1 1.0 all_to_all.55
  138.1 6.9 %all-to-all-start.1 = ((bf16[8,64,512]{2,1,0:T(8,128)(2,1)}), bf16[8,64,512]{2,1,0:T(8,128)(2,1)}, u32[]{:S(2)}, u32[]{:S(2)}) async-start(bf16[8,64,512]{2,1,0:T(8,128)(2,1)} %all_to_all.55), calls=%async_computation.1 | async-start | bytes 1048576 | tf_op jit(solution)/shard_map/all_to_all | solution.py:149
  145.1 0.3 copy.51
  145.4 1.0 all_to_all.62
  146.4 1.2 copy.57
  147.6 2.1 %copy.58 = bf16[2,1,512,128]{3,1,2,0:T(2,128)(2,1)} copy(bf16[2,1,512,128]{3,2,0,1:T(8,128)(2,1)} %bitcast.59) | data formatting | bytes 524288 | tf_op jit(solution)/shard_map/stack | solution.py:140
  149.7 2.1 %copy.59 = bf16[2,1,512,128]{3,1,2,0:T(2,128)(2,1)} copy(bf16[2,1,512,128]{3,2,0,1:T(8,128)(2,1)} %bitcast.60) | data formatting | bytes 524288 | tf_op jit(solution)/shard_map/stack | solution.py:140
  151.9 8.6 %stack.87 = bf16[2,5,512,128]{3,1,2,0:T(8,128)(2,1)S(1)} concatenate(bf16[2,1,512,128]{3,1,2,0:T(2,128)(2,1)S(1)} %get-tuple-element.20, bf16[2,1,512,128]{3,1,2,0:T(2,128)(2,1)} %copy.57, bf16[2,1,512,128]{3,1,2,0:T(2,128)(2,1)} %copy.58, bf16[2,1,512,128]{3,1,2,0:T(2,128)(2,1)} %copy.59, bf16[2,1,512,128]{3,1,2,0:T(2,128)(2,1)S(1)} %get-tuple-element.16), dimensions={1} | concatenate | bytes 2621440 | tf_op jit(solution)/shard_map/stack | solution.py:140
  160.5 5.7 %convert_bitcast_fusion = bf16[2,32,512,128]{3,1,2,0:T(8,128)(2,1)} fusion(bf16[2,5,512,128]{3,1,2,0:T(8,128)(2,1)S(1)} %stack.87, pred[5,32]{1,0:T(8,128)(4,1)S(1)} %stack.88), kind=kOutput, calls=%fused_computation.14 | convolution fusion | flops 46137344 | bytes 9699488 | tf_op jit(solution)/shard_map/np,cnbw->cpbw/dot_general | solution.py:141
  166.1 4.8 %all-to-all-start.3 = ((bf16[8,64,512]{2,1,0:T(8,128)(2,1)}), bf16[8,64,512]{2,1,0:T(8,128)(2,1)S(1)}, u32[]{:S(2)}, u32[]{:S(2)}) async-start(bf16[8,64,512]{2,1,0:T(8,128)(2,1)} %all_to_all.62), calls=%async_computation.3 | async-start | bytes 1048576 | tf_op jit(solution)/shard_map/all_to_all | solution.py:150
  170.9 4.2 %fusion.46 = (bf16[1,32,512,128]{3,1,2,0:T(8,128)(2,1)S(1)}, bf16[1,32,512,128]{3,1,2,0:T(8,128)(2,1)S(1)}) fusion(bf16[2,32,512,128]{3,1,2,0:T(8,128)(2,1)} %convert_bitcast_fusion), kind=kLoop, calls=%fused_computation.86 | loop fusion | bytes 16777216 | tf_op jit(solution)/shard_map/slice | solution.py:145
  175.2 3.6 %copy.60 = bf16[1,32,512,128]{3,2,1,0:T(8,128)(2,1)} copy(bf16[1,32,512,128]{3,1,2,0:T(8,128)(2,1)S(1)} %get-tuple-element.5) | data formatting | bytes 8388608 | tf_op jit(solution)/shard_map/slice | solution.py:144
  178.8 3.6 %copy.61 = bf16[1,32,512,128]{3,2,1,0:T(8,128)(2,1)} copy(bf16[1,32,512,128]{3,1,2,0:T(8,128)(2,1)S(1)} %get-tuple-element.4) | data formatting | bytes 8388608 | tf_op jit(solution)/shard_map/slice | solution.py:145
  182.4 1.9 %copy.74 = bf16[8,8,8,512]{3,2,0,1:T(8,128)(2,1)} copy(bf16[8,8,8,512]{3,2,1,0:T(8,128)(2,1)} %bitcast.87) | data formatting | bytes 1048576 | tf_op jit(solution)/shard_map/all_to_all | solution.py:149
  184.3 0.8 copy.75
  (42 shorter events, 0.3 us)
Async XLA Ops:
  0.6 24.8 %collective-permute-start.2 = (s32[1,4]{1,0:T(1,128)}, s32[1,4]{1,0:T(1,128)S(1)}, u32[]{:S(2)}, u32[]{:S(2)}) collective-permute-start(s32[1,4]{1,0:T(1,128)} %param.11), channel_id=1, source_target_pairs={{16,0},{24,8},{32,16},{40,24},{48,32},{56,40},{64,48},{72,56},{80,... | collective-permute-start | bytes 56 | tf_op jit(solution)/shard_map/ppermute | solution.py:15
  2.8 23.9 %collective-permute-start = (s32[1,4]{1,0:T(1,128)}, s32[1,4]{1,0:T(1,128)S(1)}, u32[]{:S(2)}, u32[]{:S(2)}) collective-permute-start(s32[1,4]{1,0:T(1,128)} %param.11), channel_id=1, source_target_pairs={{8,0},{16,8},{24,16},{32,24},{40,32},{48,40},{56,48},{64,56},{72,6... | collective-permute-start | bytes 56 | tf_op jit(solution)/shard_map/ppermute | solution.py:15
  6.4 21.5 %collective-permute-start.4 = (s32[1,4]{1,0:T(1,128)}, s32[1,4]{1,0:T(1,128)S(1)}, u32[]{:S(2)}, u32[]{:S(2)}) collective-permute-start(s32[1,4]{1,0:T(1,128)} %param.11), channel_id=1, source_target_pairs={{24,0},{32,8},{40,16},{48,24},{56,32},{64,40},{72,48},{80,56},{88,... | collective-permute-start | bytes 56 | tf_op jit(solution)/shard_map/ppermute | solution.py:15
  10.2 44.7 %all-to-all-start.2 = ((bf16[64,8,512]{2,0,1:T(8,128)(2,1)}), bf16[64,8,512]{2,0,1:T(8,128)(2,1)S(1)}, u32[]{:S(2)}, u32[]{:S(2)}) async-start(bf16[64,8,512]{2,0,1:T(8,128)(2,1)} %bitcast.181), calls=%async_computation.2 | async-start | bytes 1048576 | tf_op jit(solution)/shard_map/all_to_all | solution.py:74
  33.5 10.7 %collective-permute-start.1 = (bf16[2,512,128]{2,1,0:T(8,128)(2,1)}, bf16[2,512,128]{2,1,0:T(8,128)(2,1)}, u32[]{:S(2)}, u32[]{:S(2)}) collective-permute-start(bf16[2,512,128]{2,1,0:T(8,128)(2,1)} %pad_maximum_fusion), channel_id=1, source_target_pairs={{0,8},{8,16},{16,24},{24,32},{32,40},{40,48},{48,56},{56,64},{64,7... | collective-permute-start | bytes 786440 | tf_op jit(solution)/shard_map/ppermute | solution.py:15
  39.1 10.9 %collective-permute-start.3 = (bf16[2,512,128]{2,1,0:T(8,128)(2,1)}, bf16[2,512,128]{2,1,0:T(8,128)(2,1)}, u32[]{:S(2)}, u32[]{:S(2)}) collective-permute-start(bf16[2,512,128]{2,1,0:T(8,128)(2,1)} %pad_maximum_fusion.1), channel_id=1, source_target_pairs={{0,16},{8,24},{16,32},{24,40},{32,48},{40,56},{48,64},{56,72},{64,... | collective-permute-start | bytes 786440 | tf_op jit(solution)/shard_map/ppermute | solution.py:15
  41.1 12.7 %collective-permute-start.5 = (bf16[2,512,128]{2,1,0:T(8,128)(2,1)}, bf16[2,512,128]{2,1,0:T(8,128)(2,1)}, u32[]{:S(2)}, u32[]{:S(2)}) collective-permute-start(bf16[2,512,128]{2,1,0:T(8,128)(2,1)} %pad_maximum_fusion.2), channel_id=1, source_target_pairs={{0,24},{8,32},{16,40},{24,48},{32,56},{40,64},{48,72},{56,80},{64,... | collective-permute-start | bytes 786440 | tf_op jit(solution)/shard_map/ppermute | solution.py:15
  54.9 14.3 %all-to-all-start = ((bf16[64,8,512]{2,0,1:T(8,128)(2,1)}), bf16[64,8,512]{2,0,1:T(8,128)(2,1)}, u32[]{:S(2)}, u32[]{:S(2)}) async-start(bf16[64,8,512]{2,0,1:T(8,128)(2,1)} %bitcast.182), calls=%async_computation | async-start | bytes 1048576 | tf_op jit(solution)/shard_map/all_to_all | solution.py:73
  70.4 5.9 %copy-start.6 = (bf16[512,4,128]{2,1,0:T(4,128)(2,1)}, bf16[512,4,128]{2,1,0:T(4,128)(2,1)S(1)}, u32[]{:S(2)}) copy-start(bf16[512,4,128]{2,1,0:T(4,128)(2,1)S(1)} %reshape.228) | copy-start | bytes 1572868
  76.3 12.7 %copy-start = (f32[2560,512,4]{1,0,2:T(8,128)}, f32[2560,512,4]{1,0,2:T(8,128)S(1)}, u32[]{:S(2)}) copy-start(f32[2560,512,4]{1,0,2:T(8,128)S(1)} %get-tuple-element.28) | copy-start | bytes 62914564
  80.9 8.2 %copy-start.2 = (f32[512,1,4,128]{0,3,2,1:T(8,128)S(1)}, f32[512,1,4,128]{0,3,2,1:T(8,128)}, u32[]{:S(2)}) copy-start(f32[512,1,4,128]{0,3,2,1:T(8,128)} %copy.48) | copy-start | bytes 3145732
  80.9 8.2 %copy-start.3 = (bf16[1,5,512,128]{3,2,1,0:T(8,128)(2,1)S(1)}, bf16[1,5,512,128]{3,2,1,0:T(8,128)(2,1)}, u32[]{:S(2)}) copy-start(bf16[1,5,512,128]{3,2,1,0:T(8,128)(2,1)} %get-tuple-element.22) | copy-start | bytes 1966084
  95.9 15.7 %copy-start.7 = (bf16[512,4,128]{2,1,0:T(4,128)(2,1)S(1)}, bf16[512,4,128]{2,1,0:T(4,128)(2,1)}, u32[]{:S(2)}) copy-start(bf16[512,4,128]{2,1,0:T(4,128)(2,1)} %copy-done.6) | copy-start | bytes 1572868
  111.7 7.5 %copy-start.4 = (bf16[2560,128]{1,0:T(8,128)(2,1)S(1)}, bf16[2560,128]{1,0:T(8,128)(2,1)}, u32[]{:S(2)}) copy-start(bf16[2560,128]{1,0:T(8,128)(2,1)} %fusion.17) | copy-start | bytes 1966084
  111.7 23.6 %slice-start = ((s8[10485760]{0:T(1024)(128)(4,1)}), s8[2097152]{0:T(1024)(128)(4,1)S(1)}, s32[]{:S(2)}) async-start(s8[10485760]{0:T(1024)(128)(4,1)} %bitcast.189), calls=%async_computation.4 | async-start | bytes 4194304
  111.7 23.6 %slice-start.1 = ((s8[10485760]{0:T(1024)(128)(4,1)}), s8[4194304]{0:T(1024)(128)(4,1)S(1)}, s32[]{:S(2)}) async-start(s8[10485760]{0:T(1024)(128)(4,1)} %bitcast.189), calls=%async_computation.5 | async-start | bytes 8388608
  111.7 23.6 %copy-start.1 = (bf16[1,5,512,128]{3,2,1,0:T(8,128)(2,1)S(1)}, bf16[1,5,512,128]{3,2,1,0:T(8,128)(2,1)}, u32[]{:S(2)}) copy-start(bf16[1,5,512,128]{3,2,1,0:T(8,128)(2,1)} %get-tuple-element.21) | copy-start | bytes 1966084
  119.2 16.0 %slice-start.2 = ((s8[10485760]{0:T(1024)(128)(4,1)}), s8[4194304]{0:T(1024)(128)(4,1)S(1)}, s32[]{:S(2)}) async-start(s8[10485760]{0:T(1024)(128)(4,1)} %bitcast.189), calls=%async_computation.6 | async-start | bytes 8388608
  119.2 17.6 %copy-start.5 = (bf16[512,1,4,128]{0,3,2,1:T(8,128)(2,1)S(1)}, bf16[512,1,4,128]{0,3,2,1:T(8,128)(2,1)}, u32[]{:S(2)}) copy-start(bf16[512,1,4,128]{0,3,2,1:T(8,128)(2,1)} %get-tuple-element.30) | copy-start | bytes 1572868
  121.8 24.6 %collective-permute-start.6 = (bf16[2,512,128]{2,1,0:T(8,128)(2,1)S(1)}, bf16[2,512,128]{2,1,0:T(8,128)(2,1)S(1)}, u32[]{:S(2)}, u32[]{:S(2)}) collective-permute-start(bf16[2,512,128]{2,1,0:T(8,128)(2,1)S(1)} %bitcast.205), channel_id=1, source_target_pairs={{8,0},{16,8},{24,16},{32,24},{40,32},{48,40},{56,48},{64,56},{72,6... | collective-permute-start | bytes 786440 | tf_op jit(solution)/shard_map/ppermute | solution.py:15
  124.9 22.7 %collective-permute-start.7 = (bf16[2,512,128]{2,1,0:T(8,128)(2,1)S(1)}, bf16[2,512,128]{2,1,0:T(8,128)(2,1)}, u32[]{:S(2)}, u32[]{:S(2)}) collective-permute-start(bf16[2,512,128]{2,1,0:T(8,128)(2,1)S(1)} %bitcast.207), channel_id=1, source_target_pairs={{16,0},{24,8},{32,16},{40,24},{48,32},{56,40},{64,48},{72,56},{80,... | collective-permute-start | bytes 786440 | tf_op jit(solution)/shard_map/ppermute | solution.py:15
  131.7 18.0 %collective-permute-start.8 = (bf16[2,512,128]{2,1,0:T(8,128)(2,1)}, bf16[2,512,128]{2,1,0:T(8,128)(2,1)}, u32[]{:S(2)}, u32[]{:S(2)}) collective-permute-start(bf16[2,512,128]{2,1,0:T(8,128)(2,1)} %bitcast.183), channel_id=1, source_target_pairs={{24,0},{32,8},{40,16},{48,24},{56,32},{64,40},{72,48},{80,56},{88,... | collective-permute-start | bytes 786440 | tf_op jit(solution)/shard_map/ppermute | solution.py:15
  138.1 28.0 %all-to-all-start.1 = ((bf16[8,64,512]{2,1,0:T(8,128)(2,1)}), bf16[8,64,512]{2,1,0:T(8,128)(2,1)}, u32[]{:S(2)}, u32[]{:S(2)}) async-start(bf16[8,64,512]{2,1,0:T(8,128)(2,1)} %all_to_all.55), calls=%async_computation.1 | async-start | bytes 1048576 | tf_op jit(solution)/shard_map/all_to_all | solution.py:149
  166.1 18.2 %all-to-all-start.3 = ((bf16[8,64,512]{2,1,0:T(8,128)(2,1)}), bf16[8,64,512]{2,1,0:T(8,128)(2,1)S(1)}, u32[]{:S(2)}, u32[]{:S(2)}) async-start(bf16[8,64,512]{2,1,0:T(8,128)(2,1)} %all_to_all.62), calls=%async_computation.3 | async-start | bytes 1048576 | tf_op jit(solution)/shard_map/all_to_all | solution.py:150
where the time goes:
time: 187 us; the launch traced here: 185 us
  local copies, waits for them, and re-layouts  52.3 us (28%)
  starting transfers between devices  51.1 us (27%)
  matrix products  49.9 us (27%)
  other arithmetic  14.5 us (8%)
  waiting for transfers between devices  10.9 us (6%)
  between operations  6.36 us (3%)
    ppermute x9, starting transfers between devices, shifted(): lax.ppermute(value, axis, [(source, source + steps) for source in range(f...  27.7 us
    dot_general x1, matrix products, backward(): jnp.einsum('qhgd,khd->hgqk', grad_rows, value_rows, preferred_element_typ...  15.7 us
    another operation x4, local copies, waits for them, and re-layouts, per_device(): jnp.stack([grad_pairs[:, 0]] + returned + [grad_pairs[:, picks]], 1)  14.1 us
    dot_general x1, matrix products, backward(): jnp.einsum('hgqk,qhgd->khd', weights_low, grad_rows, preferred_element_ty...  8.15 us
    slice x2, local copies, waits for them, and re-layouts, per_device(): value_grad = placed[1].reshape(-1, feature_width)  7.84 us
    ppermute x9, waiting for transfers between devices, shifted(): lax.ppermute(value, axis, [(source, source + steps) for source in range(f...  7.7 us
    dot_general x1, matrix products, backward(): jnp.einsum('hgqk,qhgd->khd', score_grad, query_rows, preferred_element_ty...  7.02 us
    all_to_all x1, starting transfers between devices, per_device(): lax.all_to_all(attended_flat, 'head', split_axis=0, concat_axis=1, tiled=...  6.92 us
  transfers between devices with their start and end apart: 13, of which 3 were waited for; matrix products, arithmetic and copies ran while one was open for 33% of the time, Pallas kernels for 0%

commit v1 on v0

v1 whole, which is shorter than its diff:
```python
import functools

import jax
import jax.numpy as jnp
from jax import lax
from jax.experimental import pallas as pl
from jax.experimental.pallas import tpu as pltpu
from jax.sharding import PartitionSpec as P

HEAD_DIM = 128
BLOCK = 512
PICKS = 4
SLOTS = PICKS + 1
SCALE = HEAD_DIM ** -0.5
EXP2_SCALE = SCALE * 1.4426950408889634
MASKED = -1e30
MESH = pl.DeviceIdType.MESH
F32 = jnp.float32
BF16 = jnp.bfloat16


def matmul(left, right):
    return jnp.dot(left, right, preferred_element_type=F32)


def attend_kernel(
    seq_count, head_count, groups, shard_blocks,
    sel_ref, pos_ref, q_hbm, og_hbm, k_hbm, v_hbm,
    contrib, attn_recv, qgrad_recv, target_ref,
    sel_recv, k_all, v_all, q_in, og_in, q_heads, og_heads, q_t, og_t,
    key_slots, value_slots, key_t, value_t, kv_send, grad_send, expo,
    max_hist, max_run, sum_run, delta, out_acc, qgrad_acc, kgrad_acc, vgrad_acc, attn_send, qgrad_send,
    load_sem, sel_send_sem, sel_recv_sem, q_send_sem, q_recv_sem, og_send_sem, og_recv_sem,
    kv_send_sem, kv_recv_sem, grad_send_sem, grad_recv_sem, attn_send_sem, attn_recv_sem,
    qgrad_send_sem, qgrad_recv_sem, place_sem,
):
    s = lax.axis_index("seq")
    h = lax.axis_index("head")
    width = groups * HEAD_DIM
    rows = q_hbm.shape[0]

    def columns(index):
        return pl.ds(pl.multiple_of(index * width, width), width)

    def token_rows(index):
        return pl.ds(pl.multiple_of(index * rows, rows), rows)

    load_k = pltpu.make_async_copy(k_hbm, k_all, load_sem.at[0])
    load_v = pltpu.make_async_copy(v_hbm, v_all, load_sem.at[1])
    load_q = pltpu.make_async_copy(q_hbm.at[:, columns(h)], q_in.at[token_rows(h), :], load_sem.at[2])
    load_og = pltpu.make_async_copy(og_hbm.at[:, columns(h)], og_in.at[token_rows(h), :], load_sem.at[3])
    load_k.start()
    load_v.start()
    load_q.start()
    load_og.start()

    barrier = pltpu.get_barrier_semaphore()
    for step in range(1, head_count):
        peer = lax.rem(h + step, head_count)
        pl.semaphore_signal(barrier, inc=1, device_id=(s, peer), device_id_type=MESH)
    for distance in range(1, PICKS):
        for other in (lax.rem(s + distance, seq_count), lax.rem(s + seq_count - distance, seq_count)):
            pl.semaphore_signal(barrier, inc=1, device_id=(other, h), device_id_type=MESH)
    pl.semaphore_wait(barrier, head_count - 1 + 2 * (PICKS - 1))

    def sel_copy(distance):
        return pltpu.make_async_remote_copy(
            src_ref=sel_ref, dst_ref=sel_recv.at[distance - 1],
            send_sem=sel_send_sem.at[distance - 1], recv_sem=sel_recv_sem.at[distance - 1],
            device_id=(s - distance, h), device_id_type=MESH)

    for distance in range(1, PICKS):
        @pl.when(s >= distance)
        def _():
            sel_copy(distance).start()

    def token_copy(source, target, send_sem, recv_sem, step):
        peer = lax.rem(h + step, head_count)
        return pltpu.make_async_remote_copy(
            src_ref=source.at[:, columns(peer)], dst_ref=target.at[token_rows(h), :],
            send_sem=send_sem.at[step], recv_sem=recv_sem.at[step],
            device_id=(s, peer), device_id_type=MESH)

    for step in range(1, head_count):
        token_copy(q_hbm, q_in, q_send_sem, q_recv_sem, step).start()
    for step in range(1, head_count):
        token_copy(og_hbm, og_in, og_send_sem, og_recv_sem, step).start()

    load_k.wait()
    load_v.wait()

    def kv_copy(distance, kind):
        slots = (key_slots, value_slots)[kind]
        return pltpu.make_async_remote_copy(
            src_ref=kv_send.at[distance - 1, kind], dst_ref=slots.at[distance + 1],
            send_sem=kv_send_sem.at[distance - 1, kind], recv_sem=kv_recv_sem.at[distance - 1, kind],
            device_id=(s + distance, h), device_id_type=MESH)

    for distance in range(1, PICKS):
        target_ref[distance + 1] = jnp.int32(-1)

        @pl.when(s + distance < seq_count)
        def _():
            sel_copy(distance).wait_recv()
            entry = lax.rem(sel_recv[distance - 1, 0, distance], shard_blocks)
            target_ref[distance + 1] = entry
            kv_send[distance - 1, 0] = k_all[entry]
            kv_copy(distance, 0).start()
            kv_send[distance - 1, 1] = v_all[entry]
            kv_copy(distance, 1).start()

    own_entry = pos_ref[0]
    first_entry = lax.rem(sel_ref[0, 0], shard_blocks)
    target_ref[0] = own_entry
    target_ref[1] = first_entry
    key_slots[0] = k_all[own_entry]
    value_slots[0] = v_all[own_entry]
    key_slots[1] = k_all[first_entry]
    value_slots[1] = v_all[first_entry]

    load_q.wait()
    for step in range(1, head_count):
        token_copy(q_hbm, q_in, q_send_sem, q_recv_sem, step).wait_recv()
    for group in range(groups):
        piece = q_in[:, group * HEAD_DIM:(group + 1) * HEAD_DIM]
        q_heads[group] = piece
        q_t[group] = piece.T

    def transpose_slot(j):
        key_t[j] = key_slots[j].T
        value_t[j] = value_slots[j].T

    def forward_own(group, carry):
        scores = matmul(key_slots[0], q_t[group])
        key_pos = lax.broadcasted_iota(jnp.int32, scores.shape, 0)
        query_pos = lax.broadcasted_iota(jnp.int32, scores.shape, 1)
        scores = jnp.where(key_pos <= query_pos, scores, MASKED)
        new_max = jnp.max(scores, axis=0, keepdims=True)
        exponent = jnp.exp2((scores - new_max) * EXP2_SCALE)
        expo[0, group] = exponent
        max_hist[0, group] = new_max
        max_run[group] = new_max
        sum_run[group] = jnp.sum(exponent, axis=0, keepdims=True)
        out_acc[group] = matmul(value_t[0], exponent.astype(BF16))
        return carry

    transpose_slot(0)
    lax.fori_loop(0, groups, forward_own, 0)

    def forward_slot(j, carry):
        def forward_group(group, inner):
            scores = matmul(key_slots[j], q_t[group])
            old_max = max_run[group]
            new_max = jnp.maximum(old_max, jnp.max(scores, axis=0, keepdims=True))
            exponent = jnp.exp2((scores - new_max) * EXP2_SCALE)
            expo[j, group] = exponent
            max_hist[j, group] = new_max
            max_run[group] = new_max
            fade = jnp.exp2((old_max - new_max) * EXP2_SCALE)
            sum_run[group] = sum_run[group] * fade + jnp.sum(exponent, axis=0, keepdims=True)
            out_acc[group] = out_acc[group] * fade + matmul(value_t[j], exponent.astype(BF16))
            return inner

        def wait_arrival():
            for kind in range(2):
                pltpu.make_async_remote_copy(
                    src_ref=kv_send.at[j - 2, kind], dst_ref=(key_slots, value_slots)[kind].at[j],
                    send_sem=kv_send_sem.at[j - 2, kind], recv_sem=kv_recv_sem.at[j - 2, kind],
                    device_id=(s, h), device_id_type=MESH).wait_recv()

        @pl.when(s >= j - 1)
        def _():
            pl.when(j >= 2)(wait_arrival)
            transpose_slot(j)
            lax.fori_loop(0, groups, forward_group, 0)
        return carry

    lax.fori_loop(1, SLOTS, forward_slot, 0)

    load_og.wait()
    for step in range(1, head_count):
        token_copy(og_hbm, og_in, og_send_sem, og_recv_sem, step).wait_recv()

    for group in range(groups):
        piece = og_in[:, group * HEAD_DIM:(group + 1) * HEAD_DIM]
        og_heads[group] = piece
        piece_t = piece.T
        og_t[group] = piece_t
        inverse = 1.0 / sum_run[group]
        sum_run[group] = inverse
        attended = (out_acc[group] * inverse).astype(BF16)
        delta[group] = jnp.sum(piece_t.astype(F32) * attended.astype(F32), axis=0, keepdims=True)
        attn_send[:, group * HEAD_DIM:(group + 1) * HEAD_DIM] = attended.T
        qgrad_acc[group] = jnp.zeros_like(qgrad_acc[group])

    def back_copy(source, target, send_sem, recv_sem, step):
        peer = lax.rem(h + step, head_count)
        return pltpu.make_async_remote_copy(
            src_ref=source.at[token_rows(peer), :], dst_ref=target.at[:, columns(h)],
            send_sem=send_sem.at[step], recv_sem=recv_sem.at[step],
            device_id=(s, peer), device_id_type=MESH)

    def back_own(source, target, sem):
        return pltpu.make_async_copy(source.at[token_rows(h), :], target.at[:, columns(h)], sem)

    for step in range(1, head_count):
        back_copy(attn_send, attn_recv, attn_send_sem, attn_recv_sem, step).start()
    back_own(attn_send, attn_recv, place_sem.at[0]).start()

    def grad_copy(j):
        return pltpu.make_async_remote_copy(
            src_ref=grad_send.at[j], dst_ref=contrib.at[j],
            send_sem=grad_send_sem.at[j], recv_sem=grad_recv_sem.at[j],
            device_id=(s - (j - 1), h), device_id_type=MESH)

    def grad_local(j):
        return pltpu.make_async_copy(grad_send.at[j], contrib.at[j], grad_send_sem.at[j])

    def backward_slot(step, carry):
        j = SLOTS - 1 - step

        def backward_group(group, inner):
            factor = jnp.exp2((max_hist[j, group] - max_run[group]) * EXP2_SCALE) * sum_run[group]
            weights = expo[j, group] * factor
            weight_grad = matmul(value_slots[j], og_t[group])
            score_grad = (weights * (weight_grad - delta[group])).astype(BF16)
            vgrad_acc[...] += matmul(weights.astype(BF16), og_heads[group])
            kgrad_acc[...] += matmul(score_grad, q_heads[group])
            qgrad_acc[group] += matmul(key_t[j], score_grad)
            return inner

        @pl.when(s >= j - 1)
        def _():
            vgrad_acc[...] = jnp.zeros_like(vgrad_acc)
            kgrad_acc[...] = jnp.zeros_like(kgrad_acc)
            lax.fori_loop(0, groups, backward_group, 0)
            grad_send[j, 0] = (kgrad_acc[...] * SCALE).astype(BF16)
            grad_send[j, 1] = vgrad_acc[...].astype(BF16)

            @pl.when(j >= 2)
            def _():
                grad_copy(j).start()

            @pl.when(j < 2)
            def _():
                grad_local(j).start()
        return carry

    lax.fori_loop(0, SLOTS, backward_slot, 0)

    for group in range(groups):
        qgrad_send[:, group * HEAD_DIM:(group + 1) * HEAD_DIM] = (qgrad_acc[group] * SCALE).astype(BF16).T
    for step in range(1, head_count):
        back_copy(qgrad_send, qgrad_recv, qgrad_send_sem, qgrad_recv_sem, step).start()
    back_own(qgrad_send, qgrad_recv, place_sem.at[1]).start()

    for step in range(1, head_count):
        token_copy(q_hbm, q_in, q_send_sem, q_recv_sem, step).wait_send()
        token_copy(og_hbm, og_in, og_send_sem, og_recv_sem, step).wait_send()
        back_copy(attn_send, attn_recv, attn_send_sem, attn_recv_sem, step).wait()
    for distance in range(1, PICKS):
        @pl.when(s >= distance)
        def _():
            sel_copy(distance).wait_send()
            grad_copy(distance + 1).wait_send()

        @pl.when(s + distance < seq_count)
        def _():
            kv_copy(distance, 0).wait_send()
            kv_copy(distance, 1).wait_send()
            grad_copy(distance + 1).wait_recv()
    grad_local(0).wait()
    grad_local(1).wait()
    back_own(attn_send, attn_recv, place_sem.at[0]).wait()
    back_own(qgrad_send, qgrad_recv, place_sem.at[1]).wait()
    for step in range(1, head_count):
        back_copy(qgrad_send, qgrad_recv, qgrad_send_sem, qgrad_recv_sem, step).wait()


def place_kernel(
    shard_blocks, target_ref, contrib, attn_in, qgrad_in,
    attn_out, qgrad_out, key_out, value_out,
    zeros, pieces, attn_buf, qgrad_buf, zero_sem, in_sem, out_sem, piece_in_sem, piece_out_sem,
):
    outs = (key_out, value_out)
    attn_load = pltpu.make_async_copy(attn_in, attn_buf, in_sem.at[0])
    qgrad_load = pltpu.make_async_copy(qgrad_in, qgrad_buf, in_sem.at[1])
    attn_load.start()
    qgrad_load.start()

    def piece_load(slot):
        return pltpu.make_async_copy(contrib.at[slot], pieces.at[slot], piece_in_sem.at[slot])

    targets = [target_ref[slot] for slot in range(SLOTS)]
    valid = [target >= 0 for target in targets]
    for slot in range(SLOTS):
        @pl.when(valid[slot])
        def _():
            piece_load(slot).start()

    zeros[...] = jnp.zeros_like(zeros)

    def taken(block):
        hit = targets[0] == block
        for slot in range(1, SLOTS):
            hit = hit | (targets[slot] == block)
        return hit

    def rows_of(block):
        return pl.ds(pl.multiple_of(block * BLOCK, BLOCK), BLOCK)

    def zero_copy(block, kind):
        return pltpu.make_async_copy(zeros, outs[kind].at[rows_of(block), :], zero_sem.at[kind, block])

    def zero_start(block, carry):
        @pl.when(jnp.logical_not(taken(block)))
        def _():
            zero_copy(block, 0).start()
            zero_copy(block, 1).start()
        return carry

    lax.fori_loop(0, shard_blocks, zero_start, 0)

    attn_store = pltpu.make_async_copy(attn_buf, attn_out, out_sem.at[0])
    qgrad_store = pltpu.make_async_copy(qgrad_buf, qgrad_out, out_sem.at[1])
    attn_load.wait()
    attn_store.start()
    qgrad_load.wait()
    qgrad_store.start()

    for slot in range(SLOTS):
        @pl.when(valid[slot])
        def _():
            piece_load(slot).wait()

    leads = []
    for slot in range(SLOTS):
        lead = valid[slot]
        for earlier in range(slot):
            lead = lead & jnp.logical_not(targets[earlier] == targets[slot])
        leads.append(lead)

    def piece_store(slot, kind):
        return pltpu.make_async_copy(
            pieces.at[slot, kind], outs[kind].at[rows_of(targets[slot]), :], piece_out_sem.at[slot, kind])

    for slot in range(SLOTS):
        @pl.when(leads[slot])
        def _():
            repeats = jnp.int32(0)
            for later in range(slot + 1, SLOTS):
                repeats = repeats + jnp.where(targets[later] == targets[slot], 1, 0)

            @pl.when(repeats > 0)
            def _():
                total = pieces[slot].astype(F32)
                for later in range(slot + 1, SLOTS):
                    total = total + jnp.where(targets[later] == targets[slot], pieces[later].astype(F32), 0.0)
                pieces[slot] = total.astype(BF16)
            piece_store(slot, 0).start()
            piece_store(slot, 1).start()

    def zero_wait(block, carry):
        @pl.when(jnp.logical_not(taken(block)))
        def _():
            zero_copy(block, 0).wait()
            zero_copy(block, 1).wait()
        return carry

    lax.fori_loop(0, shard_blocks, zero_wait, 0)
    for slot in range(SLOTS):
        @pl.when(leads[slot])
        def _():
            piece_store(slot, 0).wait()
            piece_store(slot, 1).wait()
    attn_store.wait()
    qgrad_store.wait()


def per_device(query, keys, values, out_grad, span_pos, selected):
    seq_count = lax.axis_size("seq")
    head_count = lax.axis_size("head")
    shard_blocks = keys.shape[0] // BLOCK
    rows, features = query.shape
    width = features // head_count
    groups = width // HEAD_DIM
    any_spec = pl.BlockSpec(memory_space=pl.ANY)
    smem_spec = pl.BlockSpec(memory_space=pltpu.SMEM)
    dma = pltpu.SemaphoreType.DMA
    contrib, attn_recv, qgrad_recv, targets = pl.pallas_call(
        functools.partial(attend_kernel, seq_count, head_count, groups, shard_blocks),
        out_shape=(
            jax.ShapeDtypeStruct((SLOTS, 2, BLOCK, HEAD_DIM), BF16),
            jax.ShapeDtypeStruct(query.shape, BF16),
            jax.ShapeDtypeStruct(query.shape, BF16),
            jax.ShapeDtypeStruct((8,), jnp.int32),
        ),
        in_specs=[smem_spec, smem_spec] + [any_spec] * 4,
        out_specs=(any_spec, any_spec, any_spec, smem_spec),
        scratch_shapes=[
            pltpu.SMEM((PICKS - 1, 1, PICKS), jnp.int32),
            pltpu.VMEM((shard_blocks, BLOCK, HEAD_DIM), BF16),
            pltpu.VMEM((shard_blocks, BLOCK, HEAD_DIM), BF16),
            pltpu.VMEM((BLOCK, width), BF16),
            pltpu.VMEM((BLOCK, width), BF16),
            pltpu.VMEM((groups, BLOCK, HEAD_DIM), BF16),
            pltpu.VMEM((groups, BLOCK, HEAD_DIM), BF16),
            pltpu.VMEM((groups, HEAD_DIM, BLOCK), BF16),
            pltpu.VMEM((groups, HEAD_DIM, BLOCK), BF16),
            pltpu.VMEM((SLOTS, BLOCK, HEAD_DIM), BF16),
            pltpu.VMEM((SLOTS, BLOCK, HEAD_DIM), BF16),
            pltpu.VMEM((SLOTS, HEAD_DIM, BLOCK), BF16),
            pltpu.VMEM((SLOTS, HEAD_DIM, BLOCK), BF16),
            pltpu.VMEM((PICKS - 1, 2, BLOCK, HEAD_DIM), BF16),
            pltpu.VMEM((SLOTS, 2, BLOCK, HEAD_DIM), BF16),
            pltpu.VMEM((SLOTS, groups, BLOCK, BLOCK), F32),
            pltpu.VMEM((SLOTS, groups, 1, BLOCK), F32),
            pltpu.VMEM((groups, 1, BLOCK), F32),
            pltpu.VMEM((groups, 1, BLOCK), F32),
            pltpu.VMEM((groups, 1, BLOCK), F32),
            pltpu.VMEM((groups, HEAD_DIM, BLOCK), F32),
            pltpu.VMEM((groups, HEAD_DIM, BLOCK), F32),
            pltpu.VMEM((BLOCK, HEAD_DIM), F32),
            pltpu.VMEM((BLOCK, HEAD_DIM), F32),
            pltpu.VMEM((BLOCK, width), BF16),
            pltpu.VMEM((BLOCK, width), BF16),
            dma((4,)),
            dma((PICKS - 1,)), dma((PICKS - 1,)),
            dma((head_count,)), dma((head_count,)),
            dma((head_count,)), dma((head_count,)),
            dma((PICKS - 1, 2)), dma((PICKS - 1, 2)),
            dma((SLOTS,)), dma((SLOTS,)),
            dma((head_count,)), dma((head_count,)),
            dma((head_count,)), dma((head_count,)),
            dma((2,)),
        ],
        compiler_params=pltpu.CompilerParams(
            collective_id=0, has_side_effects=True, vmem_limit_bytes=60 * 1024 * 1024),
        name="attend",
    )(selected, span_pos, query, out_grad,
      keys.reshape(shard_blocks, BLOCK, HEAD_DIM), values.reshape(shard_blocks, BLOCK, HEAD_DIM))

    return pl.pallas_call(
        functools.partial(place_kernel, shard_blocks),
        out_shape=(
            jax.ShapeDtypeStruct(query.shape, BF16),
            jax.ShapeDtypeStruct(query.shape, BF16),
            jax.ShapeDtypeStruct(keys.shape, BF16),
            jax.ShapeDtypeStruct(values.shape, BF16),
        ),
        in_specs=[smem_spec, any_spec, any_spec, any_spec],
        out_specs=(any_spec,) * 4,
        scratch_shapes=[
            pltpu.VMEM((BLOCK, HEAD_DIM), BF16),
            pltpu.VMEM((SLOTS, 2, BLOCK, HEAD_DIM), BF16),
            pltpu.VMEM(query.shape, BF16),
            pltpu.VMEM(query.shape, BF16),
            dma((2, shard_blocks)),
            dma((2,)),
            dma((2,)),
            dma((SLOTS,)),
            dma((SLOTS, 2)),
        ],
        name="place",
    )(targets, contrib, attn_recv, qgrad_recv)


def solution(mesh):
    in_specs = (
        P(("seq", "head"), None),
        P("seq", "head"),
        P("seq", "head"),
        P(("seq", "head"), None),
        P("seq"),
        P("seq", None),
    )
    out_specs = (
        P(("seq", "head"), None),
        P(("seq", "head"), None),
        P("seq", "head"),
        P("seq", "head"),
    )
    return jax.shard_map(
        per_device, mesh=mesh, in_specs=in_specs, out_specs=out_specs, check_vma=False
    )
```

time: 187 us -> 64.4 us (0.34)
  the two profiles are of different devices: /device:TPU:109 before, /device:TPU:97 now
where the time goes in v1:
time: 64.4 us; the launch traced here: 64.3 us
  Pallas kernels  63 us (98%)
  between operations  1.29 us (2%)
    pallas_call x1, Pallas kernels, per_device(): pl.pallas_call(functools.partial(attend_kernel, seq_count, head_count, gr...  57.2 us
    pallas_call x1, Pallas kernels, per_device(): pl.pallas_call(functools.partial(place_kernel, shard_blocks), out_shape=(...  5.82 us

profile of v1, /device:TPU:97, one launch (start us, length us, event | category | flops | bytes accessed | tf_op | source)
XLA Modules:
  0.0 64.3 jit_solution(2746028721021087268)
XLA Ops:
  1.3 57.2 %attend.1 = (bf16[5,2,512,128]{3,2,1,0:T(8,128)(2,1)}, bf16[64,4096]{1,0:T(8,128)(2,1)}, bf16[64,4096]{1,0:T(8,128)(2,1)}, s32[8]{0:T(128)}) custom-call(s32[1,4]{1,0:T(1,128)} %sel_ref.1, s32[1]{0:T(128)S(6)} %copy.10.pos_ref, bf16[64,4096]{1,0:T(8,128)(2,1)} %q_hbm.1, bf16[64,4096]{1,0:T(8,128)(2,1)} %og_hbm.1, bf16[32,512,128]{2,1,0:T(8,128)(2,1)} %bitcast.2, ...), custom_call_target="tpu_custom_call" | custom-call | tf_op jit(solution)/shard_map/attend/pallas_call | solution.py:390
  58.5 5.8 %place.1 = (bf16[64,4096]{1,0:T(8,128)(2,1)}, bf16[64,4096]{1,0:T(8,128)(2,1)}, bf16[16384,128]{1,0:T(8,128)(2,1)}, bf16[16384,128]{1,0:T(8,128)(2,1)}) custom-call(s32[8]{0:T(128)} %get-tuple-element.8.target_ref, bf16[5,2,512,128]{3,2,1,0:T(8,128)(2,1)} %get-tuple-element.9.contrib, bf16[64,4096]{1,0:T(8,128)(2,1)} %get-tuple-element.10.attn_in, ...), custom_call_target="tpu_custom_call" | custom-call | tf_op jit(solution)/shard_map/place/pallas_call | solution.py:443

commit v2 on v1

v2 whole, which is shorter than its diff:
```python
import functools

import jax
import jax.numpy as jnp
from jax import lax
from jax.experimental import pallas as pl
from jax.experimental.pallas import tpu as pltpu
from jax.sharding import PartitionSpec as P

HEAD_DIM = 128
BLOCK = 512
PICKS = 4
SLOTS = PICKS + 1
RING = 4
HALVES = 2
SCALE = HEAD_DIM ** -0.5
EXP2_SCALE = SCALE * 1.4426950408889634
MASKED = -1e30
MESH = pl.DeviceIdType.MESH
F32 = jnp.float32
BF16 = jnp.bfloat16


def matmul(left, right):
    return jnp.dot(left, right, preferred_element_type=F32)


def attend_kernel(
    seq_count, head_count, groups, shard_blocks,
    sel_ref, pos_ref, q_hbm, og_hbm, k_hbm, v_hbm,
    contrib, attn_recv, qgrad_recv, target_ref,
    sel_recv, k_all, v_all, q_in, og_in, q_rows, og_rows, q_t, og_t,
    key_slots, value_slots, key_t, value_t, kv_send, grad_send, relay_kv, relay_grad, expo,
    max_hist, max_run, sum_run, delta, out_acc, qgrad_acc, weights_low, scores_low, attn_send, qgrad_send,
    load_sem, sel_send_sem, sel_recv_sem, q_send_sem, q_recv_sem, og_send_sem, og_recv_sem,
    kv_send_sem, kv_recv_sem, relay_send_sem, relay_recv_sem, pass_send_sem,
    grad_send_sem, grad_recv_sem, back_send_sem, back_recv_sem, pass_back_sem,
    attn_send_sem, attn_recv_sem, qgrad_send_sem, qgrad_recv_sem, place_sem,
):
    s = lax.axis_index("seq")
    h = lax.axis_index("head")
    width = groups * HEAD_DIM
    half = width // HALVES
    pair = groups // HALVES
    rows = q_hbm.shape[0]
    column = lax.rem(s, RING)
    relay_out = (column == RING - 1) & (s + 1 < seq_count)
    relay_in = (column == RING - 1) & (s >= RING)
    back_out = (column == 0) & (s >= RING)
    back_in = (column == 0) & (s + RING < seq_count)

    def columns(index):
        return pl.ds(pl.multiple_of(index * width, width), width)

    def half_columns(index, part):
        return pl.ds(pl.multiple_of(index * width + part * half, half), half)

    def token_rows(index):
        return pl.ds(pl.multiple_of(index * rows, rows), rows)

    load_k = pltpu.make_async_copy(k_hbm, k_all, load_sem.at[0])
    load_v = pltpu.make_async_copy(v_hbm, v_all, load_sem.at[1])
    load_q = pltpu.make_async_copy(q_hbm.at[:, columns(h)], q_in.at[token_rows(h), :], load_sem.at[2])
    load_og = pltpu.make_async_copy(og_hbm.at[:, columns(h)], og_in.at[token_rows(h), :], load_sem.at[3])
    load_q.start()
    load_k.start()
    load_v.start()
    load_og.start()

    barrier = pltpu.get_barrier_semaphore()
    for step in range(1, head_count):
        peer = lax.rem(h + step, head_count)
        pl.semaphore_signal(barrier, inc=1, device_id=(s, peer), device_id_type=MESH)
    for distance in range(1, RING + 1):
        for other in (lax.rem(s + distance, seq_count), lax.rem(s + seq_count - distance, seq_count)):
            pl.semaphore_signal(barrier, inc=1, device_id=(other, h), device_id_type=MESH)
    pl.semaphore_wait(barrier, head_count - 1 + 2 * RING)

    def remote(source, target, send_sem, recv_sem, device):
        return pltpu.make_async_remote_copy(
            src_ref=source, dst_ref=target, send_sem=send_sem, recv_sem=recv_sem,
            device_id=device, device_id_type=MESH)

    def sel_copy(distance):
        return remote(
            sel_ref, sel_recv.at[distance - 1], sel_send_sem.at[distance - 1],
            sel_recv_sem.at[distance - 1], (s - distance, h))

    for distance in range(1, PICKS):
        @pl.when(s >= distance)
        def _():
            sel_copy(distance).start()

    def q_copy(step, part):
        peer = lax.rem(h + step, head_count)
        return remote(
            q_hbm.at[:, half_columns(peer, part)], q_in.at[token_rows(h), half_columns(0, part)],
            q_send_sem.at[part, step], q_recv_sem.at[part, step], (s, peer))

    def og_copy(step):
        peer = lax.rem(h + step, head_count)
        return remote(
            og_hbm.at[:, columns(peer)], og_in.at[token_rows(h), :],
            og_send_sem.at[step], og_recv_sem.at[step], (s, peer))

    for part in range(HALVES):
        for step in range(1, head_count):
            q_copy(step, part).start()
    for step in range(1, head_count):
        og_copy(step).start()

    load_k.wait()
    load_v.wait()
    slots = (key_slots, value_slots)

    def kv_copy(distance, kind):
        return remote(
            kv_send.at[distance - 1, kind], slots[kind].at[distance + 1],
            kv_send_sem.at[distance - 1, kind], kv_recv_sem.at[distance - 1, kind], (s + distance, h))

    def relay_copy(kind):
        return remote(
            kv_send.at[0, kind], relay_kv.at[kind], relay_send_sem.at[kind], relay_recv_sem.at[kind],
            (s + RING, h))

    def pass_copy(kind):
        return remote(
            relay_kv.at[kind], slots[kind].at[2], pass_send_sem.at[kind], kv_recv_sem.at[0, kind],
            (s - (RING - 1), h))

    for distance in range(1, PICKS):
        target_ref[distance + 1] = jnp.int32(-1)

        @pl.when(s + distance < seq_count)
        def _():
            sel_copy(distance).wait_recv()
            entry = lax.rem(sel_recv[distance - 1, 0, distance], shard_blocks)
            target_ref[distance + 1] = entry
            for kind in range(2):
                kv_send[distance - 1, kind] = (k_all, v_all)[kind][entry]
                if distance == 1:
                    @pl.when(relay_out)
                    def _():
                        relay_copy(kind).start()

                    @pl.when(jnp.logical_not(relay_out))
                    def _():
                        kv_copy(1, kind).start()
                else:
                    kv_copy(distance, kind).start()

    own_entry = lax.rem(pos_ref[0], shard_blocks)
    first_entry = lax.rem(sel_ref[0, 0], shard_blocks)
    target_ref[0] = own_entry
    target_ref[1] = first_entry

    def transpose_slot(j):
        key_t[j] = key_slots[j].T
        value_t[j] = value_slots[j].T

    for j, entry in enumerate((own_entry, first_entry)):
        key_slots[j] = k_all[entry]
        value_slots[j] = v_all[entry]
        transpose_slot(j)

    def forward_first(group):
        scores = matmul(key_slots[0], q_t[group])
        key_pos = lax.broadcasted_iota(jnp.int32, scores.shape, 0)
        query_pos = lax.broadcasted_iota(jnp.int32, scores.shape, 1)
        scores = jnp.where(key_pos <= query_pos, scores, MASKED)
        new_max = jnp.max(scores, axis=0, keepdims=True)
        exponent = jnp.exp2((scores - new_max) * EXP2_SCALE)
        expo[0, group] = exponent
        max_hist[0, group] = new_max
        max_run[group] = new_max
        sum_run[group] = jnp.sum(exponent, axis=0, keepdims=True)
        out_acc[group] = matmul(value_t[0], exponent.astype(BF16))

    def forward_next(j, group):
        scores = matmul(key_slots[j], q_t[group])
        old_max = max_run[group]
        new_max = jnp.maximum(old_max, jnp.max(scores, axis=0, keepdims=True))
        exponent = jnp.exp2((scores - new_max) * EXP2_SCALE)
        expo[j, group] = exponent
        max_hist[j, group] = new_max
        max_run[group] = new_max
        fade = jnp.exp2((old_max - new_max) * EXP2_SCALE)
        sum_run[group] = sum_run[group] * fade + jnp.sum(exponent, axis=0, keepdims=True)
        out_acc[group] = out_acc[group] * fade + matmul(value_t[j], exponent.astype(BF16))

    load_q.wait()

    def local_part(part, carry):
        for step in range(1, head_count):
            q_copy(step, part).wait_recv()
        for member in range(pair):
            group = part * pair + member
            piece = q_in[:, pl.ds(pl.multiple_of(group * HEAD_DIM, HEAD_DIM), HEAD_DIM)]
            q_rows[pl.ds(pl.multiple_of(group * BLOCK, BLOCK), BLOCK), :] = piece
            q_t[group] = piece.T
        for member in range(pair):
            forward_first(part * pair + member)
        for member in range(pair):
            forward_next(1, part * pair + member)

        @pl.when(relay_in)
        def _():
            for kind in range(2):
                @pl.when(part == kind)
                def _():
                    relay_copy(kind).wait_recv()
                    pass_copy(kind).start()
        return carry

    lax.fori_loop(0, HALVES, local_part, 0)

    def forward_slot(j, carry):
        @pl.when(s >= j - 1)
        def _():
            for kind in range(2):
                remote(
                    kv_send.at[j - 2, kind], slots[kind].at[j], kv_send_sem.at[j - 2, kind],
                    kv_recv_sem.at[j - 2, kind], (s, h)).wait_recv()
            transpose_slot(j)
            for group in range(groups):
                forward_next(j, group)
        return carry

    lax.fori_loop(2, SLOTS, forward_slot, 0)

    load_og.wait()
    for step in range(1, head_count):
        og_copy(step).wait_recv()

    for group in range(groups):
        lanes = slice(group * HEAD_DIM, (group + 1) * HEAD_DIM)
        piece = og_in[:, lanes]
        og_rows[group * BLOCK:(group + 1) * BLOCK, :] = piece
        piece_t = piece.T
        og_t[group] = piece_t
        inverse = 1.0 / sum_run[group]
        sum_run[group] = inverse
        attended = (out_acc[group] * inverse).astype(BF16)
        delta[group] = jnp.sum(piece_t.astype(F32) * attended.astype(F32), axis=0, keepdims=True)
        attn_send[:, lanes] = attended.T
        qgrad_acc[group] = jnp.zeros((HEAD_DIM, BLOCK), F32)

    def attn_copy(step):
        peer = lax.rem(h + step, head_count)
        return remote(
            attn_send.at[token_rows(peer), :], attn_recv.at[:, columns(h)],
            attn_send_sem.at[step], attn_recv_sem.at[step], (s, peer))

    def qgrad_copy(step, part):
        peer = lax.rem(h + step, head_count)
        return remote(
            qgrad_send.at[token_rows(peer), half_columns(0, part)], qgrad_recv.at[:, half_columns(h, part)],
            qgrad_send_sem.at[part, step], qgrad_recv_sem.at[part, step], (s, peer))

    def own_copy(source, target, sem):
        return pltpu.make_async_copy(source.at[token_rows(h), :], target.at[:, columns(h)], sem)

    for step in range(1, head_count):
        attn_copy(step).start()
    own_copy(attn_send, attn_recv, place_sem.at[0]).start()

    def grad_copy(j, kind):
        return remote(
            grad_send.at[j, kind], contrib.at[j, kind], grad_send_sem.at[j, kind], grad_recv_sem.at[j, kind],
            (s - (j - 1), h))

    def back_copy(kind):
        return remote(
            grad_send.at[2, kind], relay_grad.at[kind], back_send_sem.at[kind], back_recv_sem.at[kind],
            (s - RING, h))

    def pass_back(kind):
        return remote(
            relay_grad.at[kind], contrib.at[2, kind], pass_back_sem.at[kind], grad_recv_sem.at[2, kind],
            (s + (RING - 1), h))

    def grad_local(j):
        return pltpu.make_async_copy(grad_send.at[j], contrib.at[j], place_sem.at[2 + j])

    def backward_tile(j, group):
        factor = jnp.exp2((max_hist[j, group] - max_run[group]) * EXP2_SCALE) * sum_run[group]
        weights = expo[j, group] * factor
        weight_grad = matmul(value_slots[j], og_t[group])
        score_grad = (weights * (weight_grad - delta[group])).astype(BF16)
        qgrad_acc[group] += matmul(key_t[j], score_grad)
        return weights.astype(BF16), score_grad

    def query_lanes(group):
        return slice(group * BLOCK, (group + 1) * BLOCK)

    def backward_slot(j, carry):
        @pl.when(s >= j - 1)
        def _():
            for group in range(groups):
                weights, score_grad = backward_tile(j, group)
                weights_low[0, :, query_lanes(group)] = weights
                scores_low[0, :, query_lanes(group)] = score_grad
            grad_send[j, 0] = (matmul(scores_low[0], q_rows[...]) * SCALE).astype(BF16)
            grad_send[j, 1] = matmul(weights_low[0], og_rows[...]).astype(BF16)
            for kind in range(2):
                @pl.when(back_out & (j == 2))
                def _():
                    back_copy(kind).start()

                @pl.when(jnp.logical_not(back_out & (j == 2)))
                def _():
                    grad_copy(j, kind).start()
        return carry

    lax.fori_loop(2, SLOTS, backward_slot, 0)

    def local_back(part, carry):
        @pl.when(back_in)
        def _():
            for kind in range(2):
                @pl.when(part == kind)
                def _():
                    back_copy(kind).wait_recv()
                    pass_back(kind).start()
        for j in range(2):
            for member in range(pair):
                group = part * pair + member
                weights, score_grad = backward_tile(j, group)
                lanes = pl.ds(pl.multiple_of(group * BLOCK, BLOCK), BLOCK)
                weights_low[j, :, lanes] = weights
                scores_low[j, :, lanes] = score_grad
        for member in range(pair):
            group = part * pair + member
            qgrad_send[:, pl.ds(pl.multiple_of(group * HEAD_DIM, HEAD_DIM), HEAD_DIM)] = (
                qgrad_acc[group] * SCALE).astype(BF16).T
        for step in range(1, head_count):
            qgrad_copy(step, part).start()
        return carry

    lax.fori_loop(0, HALVES, local_back, 0)
    own_copy(qgrad_send, qgrad_recv, place_sem.at[1]).start()
    for j in range(2):
        grad_send[j, 0] = (matmul(scores_low[j], q_rows[...]) * SCALE).astype(BF16)
        grad_send[j, 1] = matmul(weights_low[j], og_rows[...]).astype(BF16)
        grad_local(j).start()

    for step in range(1, head_count):
        og_copy(step).wait_send()
        attn_copy(step).wait()
        for part in range(HALVES):
            q_copy(step, part).wait_send()
    for distance in range(1, PICKS):
        @pl.when(s >= distance)
        def _():
            sel_copy(distance).wait_send()
    for kind in range(2):
        @pl.when(relay_out)
        def _():
            relay_copy(kind).wait_send()

        @pl.when(jnp.logical_not(relay_out) & (s + 1 < seq_count))
        def _():
            kv_copy(1, kind).wait_send()

        @pl.when(relay_in)
        def _():
            pass_copy(kind).wait_send()

        @pl.when(back_out)
        def _():
            back_copy(kind).wait_send()

        @pl.when(jnp.logical_not(back_out) & (s >= 1))
        def _():
            grad_copy(2, kind).wait_send()

        @pl.when(back_in)
        def _():
            pass_back(kind).wait_send()

        for distance in range(2, PICKS):
            @pl.when(s + distance < seq_count)
            def _():
                kv_copy(distance, kind).wait_send()

            @pl.when(s >= distance)
            def _():
                grad_copy(distance + 1, kind).wait_send()
        for distance in range(1, PICKS):
            @pl.when(s + distance < seq_count)
            def _():
                grad_copy(distance + 1, kind).wait_recv()
    grad_local(0).wait()
    grad_local(1).wait()
    own_copy(attn_send, attn_recv, place_sem.at[0]).wait()
    own_copy(qgrad_send, qgrad_recv, place_sem.at[1]).wait()
    for part in range(HALVES):
        for step in range(1, head_count):
            qgrad_copy(step, part).wait()


def place_kernel(
    shard_blocks, target_ref, contrib, attn_in, qgrad_in,
    attn_out, qgrad_out, key_out, value_out,
    zeros, pieces, attn_buf, qgrad_buf, zero_sem, in_sem, out_sem, piece_in_sem, piece_out_sem,
):
    outs = (key_out, value_out)
    attn_load = pltpu.make_async_copy(attn_in, attn_buf, in_sem.at[0])
    qgrad_load = pltpu.make_async_copy(qgrad_in, qgrad_buf, in_sem.at[1])
    attn_load.start()
    qgrad_load.start()

    def piece_load(slot):
        return pltpu.make_async_copy(contrib.at[slot], pieces.at[slot], piece_in_sem.at[slot])

    targets = [target_ref[slot] for slot in range(SLOTS)]
    valid = [target >= 0 for target in targets]
    for slot in range(SLOTS):
        @pl.when(valid[slot])
        def _():
            piece_load(slot).start()

    zeros[...] = jnp.zeros_like(zeros)

    def taken(block):
        hit = targets[0] == block
        for slot in range(1, SLOTS):
            hit = hit | (targets[slot] == block)
        return hit

    def rows_of(block):
        return pl.ds(pl.multiple_of(block * BLOCK, BLOCK), BLOCK)

    def zero_copy(block, kind):
        return pltpu.make_async_copy(zeros, outs[kind].at[rows_of(block), :], zero_sem.at[kind, block])

    def zero_start(block, carry):
        @pl.when(jnp.logical_not(taken(block)))
        def _():
            zero_copy(block, 0).start()
            zero_copy(block, 1).start()
        return carry

    lax.fori_loop(0, shard_blocks, zero_start, 0)

    attn_store = pltpu.make_async_copy(attn_buf, attn_out, out_sem.at[0])
    qgrad_store = pltpu.make_async_copy(qgrad_buf, qgrad_out, out_sem.at[1])
    attn_load.wait()
    attn_store.start()
    qgrad_load.wait()
    qgrad_store.start()

    for slot in range(SLOTS):
        @pl.when(valid[slot])
        def _():
            piece_load(slot).wait()

    leads = []
    for slot in range(SLOTS):
        lead = valid[slot]
        for earlier in range(slot):
            lead = lead & jnp.logical_not(targets[earlier] == targets[slot])
        leads.append(lead)

    def piece_store(slot, kind):
        return pltpu.make_async_copy(
            pieces.at[slot, kind], outs[kind].at[rows_of(targets[slot]), :], piece_out_sem.at[slot, kind])

    for slot in range(SLOTS):
        @pl.when(leads[slot])
        def _():
            repeats = jnp.int32(0)
            for later in range(slot + 1, SLOTS):
                repeats = repeats + jnp.where(targets[later] == targets[slot], 1, 0)

            @pl.when(repeats > 0)
            def _():
                total = pieces[slot].astype(F32)
                for later in range(slot + 1, SLOTS):
                    total = total + jnp.where(targets[later] == targets[slot], pieces[later].astype(F32), 0.0)
                pieces[slot] = total.astype(BF16)
            piece_store(slot, 0).start()
            piece_store(slot, 1).start()

    def zero_wait(block, carry):
        @pl.when(jnp.logical_not(taken(block)))
        def _():
            zero_copy(block, 0).wait()
            zero_copy(block, 1).wait()
        return carry

    lax.fori_loop(0, shard_blocks, zero_wait, 0)
    for slot in range(SLOTS):
        @pl.when(leads[slot])
        def _():
            piece_store(slot, 0).wait()
            piece_store(slot, 1).wait()
    attn_store.wait()
    qgrad_store.wait()


def per_device(query, keys, values, out_grad, span_pos, selected):
    seq_count = lax.axis_size("seq")
    head_count = lax.axis_size("head")
    shard_blocks = keys.shape[0] // BLOCK
    rows, features = query.shape
    width = features // head_count
    groups = width // HEAD_DIM
    any_spec = pl.BlockSpec(memory_space=pl.ANY)
    smem_spec = pl.BlockSpec(memory_space=pltpu.SMEM)
    dma = pltpu.SemaphoreType.DMA
    contrib, attn_recv, qgrad_recv, targets = pl.pallas_call(
        functools.partial(attend_kernel, seq_count, head_count, groups, shard_blocks),
        out_shape=(
            jax.ShapeDtypeStruct((SLOTS, 2, BLOCK, HEAD_DIM), BF16),
            jax.ShapeDtypeStruct(query.shape, BF16),
            jax.ShapeDtypeStruct(query.shape, BF16),
            jax.ShapeDtypeStruct((8,), jnp.int32),
        ),
        in_specs=[smem_spec, smem_spec] + [any_spec] * 4,
        out_specs=(any_spec, any_spec, any_spec, smem_spec),
        scratch_shapes=[
            pltpu.SMEM((PICKS - 1, 1, PICKS), jnp.int32),
            pltpu.VMEM((shard_blocks, BLOCK, HEAD_DIM), BF16),
            pltpu.VMEM((shard_blocks, BLOCK, HEAD_DIM), BF16),
            pltpu.VMEM((BLOCK, width), BF16),
            pltpu.VMEM((BLOCK, width), BF16),
            pltpu.VMEM((groups * BLOCK, HEAD_DIM), BF16),
            pltpu.VMEM((groups * BLOCK, HEAD_DIM), BF16),
            pltpu.VMEM((groups, HEAD_DIM, BLOCK), BF16),
            pltpu.VMEM((groups, HEAD_DIM, BLOCK), BF16),
            pltpu.VMEM((SLOTS, BLOCK, HEAD_DIM), BF16),
            pltpu.VMEM((SLOTS, BLOCK, HEAD_DIM), BF16),
            pltpu.VMEM((SLOTS, HEAD_DIM, BLOCK), BF16),
            pltpu.VMEM((SLOTS, HEAD_DIM, BLOCK), BF16),
            pltpu.VMEM((PICKS - 1, 2, BLOCK, HEAD_DIM), BF16),
            pltpu.VMEM((SLOTS, 2, BLOCK, HEAD_DIM), BF16),
            pltpu.VMEM((2, BLOCK, HEAD_DIM), BF16),
            pltpu.VMEM((2, BLOCK, HEAD_DIM), BF16),
            pltpu.VMEM((SLOTS, groups, BLOCK, BLOCK), F32),
            pltpu.VMEM((SLOTS, groups, 1, BLOCK), F32),
            pltpu.VMEM((groups, 1, BLOCK), F32),
            pltpu.VMEM((groups, 1, BLOCK), F32),
            pltpu.VMEM((groups, 1, BLOCK), F32),
            pltpu.VMEM((groups, HEAD_DIM, BLOCK), F32),
            pltpu.VMEM((groups, HEAD_DIM, BLOCK), F32),
            pltpu.VMEM((2, BLOCK, groups * BLOCK), BF16),
            pltpu.VMEM((2, BLOCK, groups * BLOCK), BF16),
            pltpu.VMEM((BLOCK, width), BF16),
            pltpu.VMEM((BLOCK, width), BF16),
            dma((4,)),
            dma((PICKS - 1,)), dma((PICKS - 1,)),
            dma((HALVES, head_count)), dma((HALVES, head_count)),
            dma((head_count,)), dma((head_count,)),
            dma((PICKS - 1, 2)), dma((PICKS - 1, 2)),
            dma((2,)), dma((2,)), dma((2,)),
            dma((SLOTS, 2)), dma((SLOTS, 2)),
            dma((2,)), dma((2,)), dma((2,)),
            dma((head_count,)), dma((head_count,)),
            dma((HALVES, head_count)), dma((HALVES, head_count)),
            dma((4,)),
        ],
        compiler_params=pltpu.CompilerParams(
            collective_id=0, has_side_effects=True, vmem_limit_bytes=56 * 1024 * 1024),
        name="attend",
    )(selected, span_pos, query, out_grad,
      keys.reshape(shard_blocks, BLOCK, HEAD_DIM), values.reshape(shard_blocks, BLOCK, HEAD_DIM))

    return pl.pallas_call(
        functools.partial(place_kernel, shard_blocks),
        out_shape=(
            jax.ShapeDtypeStruct(query.shape, BF16),
            jax.ShapeDtypeStruct(query.shape, BF16),
            jax.ShapeDtypeStruct(keys.shape, BF16),
            jax.ShapeDtypeStruct(values.shape, BF16),
        ),
        in_specs=[smem_spec, any_spec, any_spec, any_spec],
        out_specs=(any_spec,) * 4,
        scratch_shapes=[
            pltpu.VMEM((BLOCK, HEAD_DIM), BF16),
            pltpu.VMEM((SLOTS, 2, BLOCK, HEAD_DIM), BF16),
            pltpu.VMEM(query.shape, BF16),
            pltpu.VMEM(query.shape, BF16),
            dma((2, shard_blocks)),
            dma((2,)),
            dma((2,)),
            dma((SLOTS,)),
            dma((SLOTS, 2)),
        ],
        name="place",
    )(targets, contrib, attn_recv, qgrad_recv)


def solution(mesh):
    in_specs = (
        P(("seq", "head"), None),
        P("seq", "head"),
        P("seq", "head"),
        P(("seq", "head"), None),
        P("seq"),
        P("seq", None),
    )
    out_specs = (
        P(("seq", "head"), None),
        P(("seq", "head"), None),
        P("seq", "head"),
        P("seq", "head"),
    )
    return jax.shard_map(
        per_device, mesh=mesh, in_specs=in_specs, out_specs=out_specs, check_vma=False
    )
```

time: 64.4 us -> 62 us (0.963)
  the two profiles are of different devices: /device:TPU:97 before, /device:TPU:34 now
where the time goes in v2:
time: 62 us; the launch traced here: 61.8 us
  Pallas kernels  60.5 us (98%)
  between operations  1.29 us (2%)
    pallas_call x1, Pallas kernels, per_device(): pl.pallas_call(functools.partial(attend_kernel, seq_count, head_count, gr...  54.9 us
    pallas_call x1, Pallas kernels, per_device(): pl.pallas_call(functools.partial(place_kernel, shard_blocks), out_shape=(...  5.67 us

profile of v2, /device:TPU:34, one launch (start us, length us, event | category | flops | bytes accessed | tf_op | source)
XLA Modules:
  0.0 61.8 jit_solution(9374053031779457796)
XLA Ops:
  1.3 54.9 %attend.1 = (bf16[5,2,512,128]{3,2,1,0:T(8,128)(2,1)}, bf16[64,4096]{1,0:T(8,128)(2,1)}, bf16[64,4096]{1,0:T(8,128)(2,1)}, s32[8]{0:T(128)}) custom-call(s32[1,4]{1,0:T(1,128)} %sel_ref.1, s32[1]{0:T(128)S(6)} %copy.10.pos_ref, bf16[64,4096]{1,0:T(8,128)(2,1)} %q_hbm.1, bf16[64,4096]{1,0:T(8,128)(2,1)} %og_hbm.1, bf16[32,512,128]{2,1,0:T(8,128)(2,1)} %bitcast.2, ...), custom_call_target="tpu_custom_call" | custom-call | tf_op jit(solution)/shard_map/attend/pallas_call | solution.py:512
  56.2 5.7 %place.1 = (bf16[64,4096]{1,0:T(8,128)(2,1)}, bf16[64,4096]{1,0:T(8,128)(2,1)}, bf16[16384,128]{1,0:T(8,128)(2,1)}, bf16[16384,128]{1,0:T(8,128)(2,1)}) custom-call(s32[8]{0:T(128)} %get-tuple-element.8.target_ref, bf16[5,2,512,128]{3,2,1,0:T(8,128)(2,1)} %get-tuple-element.9.contrib, bf16[64,4096]{1,0:T(8,128)(2,1)} %get-tuple-element.10.attn_in, ...), custom_call_target="tpu_custom_call" | custom-call | tf_op jit(solution)/shard_map/place/pallas_call | solution.py:569
